TPU v7x, 256 devices: a whole 4x4x8 slice. The times are simulated.
256 devices in a mesh: row: 32 (over z, y), col: 8 (over x, core).
Axes of the slice: x: 4, y: 4, z: 8, core: 2. Of those that a mesh axis runs over, the one named last changes fastest.
Arguments:
- feats: bfloat16 [131072, 256], P(('row', 'col')), may hold values from -6 to 6
- w_msg: bfloat16 [256, 256], replicated, may hold values from -0.375 to 0.375
- w_self: bfloat16 [256, 256], replicated, may hold values from -0.375 to 0.375
- bias: float32 [256], replicated, may hold values from -3 to 3
- hit_mask: int32 [131072], P(('row', 'col')), may hold values 0 or 1
- block_cols: int32 [32, 8, 96], P('row', 'col'), may hold values from 0 to 127, as said below
- block_count: int32 [32, 8], P('row', 'col'), may hold values from 32 to 96, as said below
- edge_vals: bfloat16 [32, 8, 96, 128, 128], P('row', 'col'), may hold values from -0.125 to 0.125
- grad_out: bfloat16 [131072, 256], P(('row', 'col')), may hold values from -3 to 3
Outputs:
- hidden: bfloat16 [131072, 256], P(('row', 'col'))
- grad_feats: bfloat16 [131072, 256], P(('row', 'col'))
- edge_grad: bfloat16 [32, 8, 96, 128, 128], P('row', 'col')
- w_msg_grad: float32 [256, 256], replicated
- w_self_grad: float32 [256, 256], replicated
- bias_grad: float32 [256], replicated
Inputs may be any that keep to these rules, and one draw needn't show every extreme that they name: `block_cols`: slot s of a tile serves the tile's local block row s % 32; the block columns of the slots that serve one block row of one tile are different. Slots from block_count on are unused.
All inputs are finite; a program needn't handle non-finite values. No bound on the sum of `hit_mask` on one device may be relied on, other than what follows from the above.
Results may differ from a plain program's by a relative error of at most 0.015.
Values may be sent and summed in bfloat16 or wider, within the bound.
A program may use at most 128 MiB of HBM per device.

v0:
```python
import math
import jax
import jax.numpy as jnp
from jax import lax
from jax.sharding import PartitionSpec as P


def activate(pre, row_mask, grad_in):
    sig = jax.nn.sigmoid(pre)
    hidden = (pre * sig * row_mask).astype(jnp.bfloat16)
    deriv = sig * (1.0 + pre * (1.0 - sig))
    grad_pre = (grad_in.astype(jnp.float32) * row_mask * deriv).astype(jnp.bfloat16)
    return (hidden, grad_pre)


def per_device(feats, w_msg, w_self, bias, hit_mask, block_cols, block_count, edge_vals, grad_out):
    row_count = lax.axis_size("row")
    col_count = lax.axis_size("col")
    own_rows = feats.shape[0]
    width = feats.shape[1]
    row_mask = hit_mask.astype(jnp.float32)[:, None]
    messages = (jnp.dot(feats, w_msg, preferred_element_type=jnp.float32) * row_mask).astype(
        jnp.bfloat16
    )
    column_msgs = lax.all_gather(messages, "row", axis=0, tiled=True)
    slot_cols = block_cols[0, 0]
    edge_block = edge_vals[0, 0]
    slot_total = edge_block.shape[0]
    edge_size = edge_block.shape[1]
    tile_rows = col_count * own_rows // edge_size
    tile_cols = row_count * own_rows // edge_size
    slot_depth = slot_total // tile_rows
    slot_flags = jnp.arange(slot_total, dtype=jnp.int32) < block_count[0, 0]
    edge_live = (edge_block * slot_flags.astype(jnp.bfloat16)[:, None, None]).reshape(
        slot_depth, tile_rows, edge_size, edge_size
    )
    col_blocks = column_msgs.reshape(tile_cols, edge_size, width)[slot_cols].reshape(
        slot_depth, tile_rows, edge_size, width
    )
    partial_value = jnp.einsum(
        "krij,krjf->rif", edge_live, col_blocks, preferred_element_type=jnp.float32
    ).reshape(tile_rows * edge_size, width)
    summed = lax.psum_scatter(
        partial_value.astype(jnp.bfloat16), "col", scatter_dimension=0, tiled=True
    ).astype(jnp.float32)
    pre = summed + jnp.dot(feats, w_self, preferred_element_type=jnp.float32) + bias
    hidden, grad_pre = activate(pre, row_mask, grad_out)
    grad_rows_all = lax.all_gather(grad_pre, "col", axis=0, tiled=True)
    grad_tile = grad_rows_all.reshape(tile_rows, edge_size, width)
    backward = jnp.einsum(
        "krij,rif->krjf", edge_live, grad_tile, preferred_element_type=jnp.float32
    ).reshape(slot_total, edge_size, width)
    back_part = jax.ops.segment_sum(backward, slot_cols, num_segments=tile_cols).reshape(
        tile_cols * edge_size, width
    )
    edge_grad = (
        jnp.einsum(
            "rif,krjf->krij", grad_tile, col_blocks, preferred_element_type=jnp.float32
        ).reshape(slot_total, edge_size, edge_size)
        * slot_flags.astype(jnp.float32)[:, None, None]
    ).astype(jnp.bfloat16)
    grad_sum = lax.psum_scatter(
        back_part.astype(jnp.bfloat16), "row", scatter_dimension=0, tiled=True
    ).astype(jnp.float32)
    grad_msg = (grad_sum * row_mask).astype(jnp.bfloat16)
    grad_feats = (
        jnp.einsum("hg,fg->hf", grad_msg, w_msg, preferred_element_type=jnp.float32)
        + jnp.einsum("hg,fg->hf", grad_pre, w_self, preferred_element_type=jnp.float32)
    ).astype(jnp.bfloat16)
    local_msg = jnp.einsum("hf,hg->fg", feats, grad_msg, preferred_element_type=jnp.float32)
    local_self = jnp.einsum("hf,hg->fg", feats, grad_pre, preferred_element_type=jnp.float32)
    local_bias = jnp.sum(grad_pre.astype(jnp.float32), axis=0)
    total_msg, total_self, total_bias = lax.psum(
        (local_msg, local_self, local_bias), ("row", "col")
    )
    factor = 1.0 / math.sqrt(own_rows * row_count * col_count)
    return (
        hidden,
        grad_feats,
        edge_grad[None, None],
        total_msg * factor,
        total_self * factor,
        total_bias * factor,
    )


def solution(mesh):
    placed = (
        P(("row", "col"), None),
        P(),
        P(),
        P(),
        P(("row", "col")),
        P("row", "col", None),
        P("row", "col"),
        P("row", "col", None, None, None),
        P(("row", "col"), None),
    )
    return jax.shard_map(
        per_device,
        mesh=mesh,
        in_specs=placed,
        out_specs=(
            P(("row", "col"), None),
            P(("row", "col"), None),
            P("row", "col", None, None, None),
            P(),
            P(),
            P(),
        ),
        check_vma=False,
    )
```

profile of v0, /device:TPU:2, one launch (start us, length us, event | category | flops | bytes accessed | tf_op | source)
XLA Modules:
  0.0 757.9 jit_solution(17679265204071514697)
XLA Ops:
  7.2 0.0 copy-start
  7.2 0.0 all-gather.3.cloned.1.call-start
  7.2 0.7 convert_element_type.67
  7.9 0.2 copy-done
  8.1 1.8 fusion.12
  10.0 0.0 all-gather.3.cloned.1.call-update
  10.0 0.0 reduce-scatter.3.cloned.1.call-start
  10.7 0.7 fusion.16
  11.4 100.7 %all-gather.3.cloned.1.call-done = bf16[16384,256]{1,0:T(8,128)(2,1)} async-done(((bf16[512,256]{1,0:T(8,128)(2,1)}), bf16[16384,256]{1,0:T(8,128)(2,1)}) %all-gather.3.cloned.1.call-update) | async-done | bytes 8388624 | tf_op jit(solution)/shard_map/all_gather | solution.py:25
  112.0 0.0 copy-start.2
  112.0 9.5 %gather_fusion = bf16[96,128,256]{2,1,0:T(8,128)(2,1)} fusion(bf16[128,128,256]{2,1,0:T(8,128)(2,1)} %bitcast.53, s32[1024]{0:T(1024)S(1)} %pad_clamp_fusion), kind=kCustom, calls=%fused_computation | custom fusion | bytes 12583296 | tf_op jit(solution)/shard_map/gather | solution.py:37
  121.5 0.0 copy-done.2
  121.5 0.0 copy-start.5
  121.5 5.5 bitcast_convert_fusion
  127.0 0.0 reduce-scatter.3.cloned.1.call-update
  127.0 0.0 all-gather.5.cloned.1.call-start
  127.1 30.4 %reduce-scatter.3.cloned.1.call-done = bf16[512,256]{1,0:T(8,128)(2,1)} async-done(((bf16[4096,256]{1,0:T(8,128)(2,1)}), bf16[512,256]{1,0:T(8,128)(2,1)}) %reduce-scatter.3.cloned.1.call-update) | async-done | bytes 262160 | tf_op jit(solution)/shard_map/reduce_scatter | solution.py:43
  157.5 0.0 copy-done.5
  157.5 2.3 convert_reduce_fusion
  159.8 0.0 all-gather.5.cloned.1.call-update
  159.8 0.0 reduce-scatter.5.cloned.1.call-start
  159.9 28.7 %all-gather.5.cloned.1.call-done = bf16[4096,256]{1,0:T(8,128)(2,1)} async-done(((bf16[512,256]{1,0:T(8,128)(2,1)}), bf16[4096,256]{1,0:T(8,128)(2,1)}) %all-gather.5.cloned.1.call-update) | async-done | bytes 2097168 | tf_op jit(solution)/shard_map/all_gather | solution.py:48
  188.6 8.0 %convolution_bitcast_fusion = f32[3,32,128,256]{2,3,0,1:T(8,128)} fusion(bf16[32,128,256,1]{2,1,3,0:T(8,128)(2,1)} %bitcast.51, bf16[3,32,128,128]{3,2,1,0:T(8,128)(2,1)S(1)} %bitcast.55, bf16[3,32]{0,1:T(8,128)(2,1)S(1)} %fusion.15), kind=kOutput, calls=%fused_computation.7 | convolution fusion | flops 811597824 | bytes 17825984 | tf_op jit(solution)/shard_map/krij,rif->krjf/dot_general | solution.py:50
  196.6 12.6 %copy.22 = f32[3,32,128,256]{3,2,1,0:T(8,128)} copy(f32[3,32,128,256]{2,3,0,1:T(8,128)} %convolution_bitcast_fusion) | data formatting | bytes 25165824 | tf_op jit(solution)/shard_map/krij,rif->krjf/transpose | solution.py:50
  209.2 7.8 %broadcast_in_dim.2 = f32[128,128,256]{2,1,0:T(8,128)} broadcast(f32[]{:T(128)} %constant.4.clone.1), dimensions={} | broadcast | bytes 16777220 | tf_op jit(solution)/shard_map/broadcast_in_dim | solution.py:53
  217.0 0.0 copy-done.6
  217.0 29.1 %scatter_fusion = f32[128,128,256]{2,1,0:T(8,128)} fusion(f32[128,128,256]{2,1,0:T(8,128)} %broadcast_in_dim.2, s32[96]{0:T(128)S(1)} %bitcast.57, f32[96,128,256]{2,1,0:T(8,128)} %bitcast.46), kind=kCustom, calls=%fused_computation.1 | custom fusion | flops 3145728 | bytes 37749120 | tf_op jit(solution)/shard_map/scatter-add | solution.py:53
  246.1 9.0 %convert_element_type.75 = bf16[128,128,256]{2,1,0:T(8,128)(2,1)} convert(f32[128,128,256]{2,1,0:T(8,128)} %scatter_fusion) | non-fusion elementwise | flops 4194304 | bytes 25165824 | tf_op jit(solution)/shard_map/convert_element_type | solution.py:63
  255.1 0.0 reduce-scatter.5.cloned.1.call-update
  255.2 0.0 all-reduce.3.cloned.1.call-start
  255.2 78.1 %psum.23 = f32[256]{0:T(256)S(1)} all-reduce(f32[256]{0:T(256)S(1)} %get-tuple-element.20), channel_id=1, replica_groups=mesh['row'=32,'col'=8] {'row','col'}, use_global_device_ids=true, to_apply=%region_6.0 | all-reduce | flops 256 | bytes 2048 | tf_op jit(solution)/shard_map/psum | solution.py:73
  333.3 0.6 broadcast_multiply_fusion.2
  333.9 0.0 copy-done.3
  333.9 1.0 convolution_bitcast_fusion.1
  334.9 0.0 copy-done.1
  334.9 7.3 fusion.4
  342.1 6.6 copy.24
  348.7 5.1 multiply_convert_fusion
  353.8 134.4 %reduce-scatter.5.cloned.1.call-done = bf16[512,256]{1,0:T(8,128)(2,1)} async-done(((bf16[16384,256]{1,0:T(8,128)(2,1)}), bf16[512,256]{1,0:T(8,128)(2,1)}) %reduce-scatter.5.cloned.1.call-update) | async-done | bytes 262160 | tf_op jit(solution)/shard_map/reduce_scatter | solution.py:62
  488.2 2.0 convolution_bitcast_fusion.2
  490.2 0.0 all-reduce.3.cloned.1.call-update
  490.2 0.0 copy-done.4
  490.2 1.2 fusion.14
  491.4 1.0 fusion.13
  492.4 256.2 %all-reduce.3.cloned.1.call-done = (f32[256,256]{0,1:T(8,128)}, f32[256,256]{0,1:T(8,128)}) async-done(((f32[256,256]{0,1:T(8,128)}, f32[256,256]{0,1:T(8,128)}), (f32[256,256]{0,1:T(8,128)}, f32[256,256]{0,1:T(8,128)})) %all-reduce.3.cloned.1.call-update) | async-done | bytes 524304 | tf_op jit(solution)/shard_map/psum | solution.py:73
  748.6 1.1 broadcast_multiply_fusion
  749.7 0.8 copy.26
  750.5 0.8 copy.25
  (7 shorter events, 0.0 us)
Async XLA Ops:
  7.2 1.0 copy-start
  7.2 104.8 %all-gather.3.cloned.1.call-start = ((), (), s32[]{:S(2)}) async-start(), calls=%async_computation.2 | async-start | bytes 8650752 | tf_op jit(solution)/shard_map/all_gather | solution.py:25
  10.0 147.5 %reduce-scatter.3.cloned.1.call-start = ((), (), s32[]{:S(2)}) async-start(), calls=%async_computation.3 | async-start | bytes 2359296 | tf_op jit(solution)/shard_map/reduce_scatter | solution.py:43
  112.0 9.5 %copy-start.2 = (bf16[1,1,96,128,128]{4,3,2,1,0:T(8,128)(2,1)S(1)}, bf16[1,1,96,128,128]{4,3,2,1,0:T(8,128)(2,1)}, u32[]{:S(2)}) copy-start(bf16[1,1,96,128,128]{4,3,2,1,0:T(8,128)(2,1)} %param.16) | copy-start | bytes 9437188
  121.5 36.0 %copy-start.5 = (bf16[256,256]{1,0:T(8,128)(2,1)S(1)}, bf16[256,256]{1,0:T(8,128)(2,1)}, u32[]{:S(2)}) copy-start(bf16[256,256]{1,0:T(8,128)(2,1)} %param.11) | copy-start | bytes 393220
  127.0 61.6 %all-gather.5.cloned.1.call-start = ((), (), s32[]{:S(2)}) async-start(), calls=%async_computation.4 | async-start | bytes 2359296 | tf_op jit(solution)/shard_map/all_gather | solution.py:48
  159.8 328.4 %reduce-scatter.5.cloned.1.call-start = ((), (), s32[]{:S(2)}) async-start(), calls=%async_computation.5 | async-start | bytes 8650752 | tf_op jit(solution)/shard_map/reduce_scatter | solution.py:62
  209.2 7.9 %copy-start.6 = (s32[1,1,96]{2,1,0:T(1,128)S(1)}, s32[1,1,96]{2,1,0:T(1,128)}, u32[]{:S(2)}) copy-start(s32[1,1,96]{2,1,0:T(1,128)} %param.14) | copy-start | bytes 1156
  255.1 78.7 %copy-start.3 = (bf16[512,256]{1,0:T(8,128)(2,1)S(1)}, bf16[512,256]{1,0:T(8,128)(2,1)}, u32[]{:S(2)}) copy-start(bf16[512,256]{1,0:T(8,128)(2,1)} %get-tuple-element.21) | copy-start | bytes 786436
  255.1 79.7 %copy-start.1 = (bf16[4096,256]{1,0:T(8,128)(2,1)S(1)}, bf16[4096,256]{1,0:T(8,128)(2,1)}, u32[]{:S(2)}) copy-start(bf16[4096,256]{1,0:T(8,128)(2,1)} %all-gather.5.cloned.1.call-done) | copy-start | bytes 6291460
  255.2 493.4 %all-reduce.3.cloned.1.call-start = ((), (), s32[]{:S(2)}) async-start(), calls=%async_computation.6 | async-start | bytes 1048576 | tf_op jit(solution)/shard_map/psum | solution.py:73
  348.7 141.5 %copy-start.4 = (bf16[256,256]{1,0:T(8,128)(2,1)S(1)}, bf16[256,256]{1,0:T(8,128)(2,1)}, u32[]{:S(2)}) copy-start(bf16[256,256]{1,0:T(8,128)(2,1)} %param.10) | copy-start | bytes 393220
Sparse Core Ops, SparseCore 0:
  11.1 100.8 all-gather.2
  127.1 30.3 reduce-scatter.2
  159.9 28.6 all-gather.4
  255.3 232.8 reduce-scatter.4
  494.2 254.3 all-reduce.2
where the time goes:
time: 758 us
  waiting for transfers between devices  550 us (73%)
  blocking collectives  78.1 us (10%)
  other arithmetic  46.2 us (6%)
  local copies, waits for them, and re-layouts  38.4 us (5%)
  matrix products  30 us (4%)
  between operations  14.5 us (2%)
    psum x1, waiting for transfers between devices, per_device(): lax.psum((local_msg, local_self, local_bias), ('row', 'col'))  256 us
    reduce_scatter x1, waiting for transfers between devices, per_device(): lax.psum_scatter(back_part.astype(jnp.bfloat16), 'row', scatter_dimension...  134 us
    all_gather x1, waiting for transfers between devices, per_device(): column_msgs = lax.all_gather(messages, 'row', axis=0, tiled=True)  101 us
    psum x1, blocking collectives, per_device(): lax.psum((local_msg, local_self, local_bias), ('row', 'col'))  78.1 us
    reduce_scatter x1, waiting for transfers between devices, per_device(): lax.psum_scatter(partial_value.astype(jnp.bfloat16), 'col', scatter_dimen...  30.4 us
    scatter-add x1, other arithmetic, per_device(): jax.ops.segment_sum(backward, slot_cols, num_segments=tile_cols)  29.1 us
    all_gather x1, waiting for transfers between devices, per_device(): grad_rows_all = lax.all_gather(grad_pre, 'col', axis=0, tiled=True)  28.7 us
  transfers between devices with their start and end apart: 5, of which 5 were waited for; matrix products, arithmetic and copies ran while one was open for 3% of the time, Pallas kernels for 0%

commit v1 on v0

--- a/solution.py
+++ b/solution.py
@@ -71,7 +71,7 @@
     local_self = jnp.einsum("hf,hg->fg", feats, grad_pre, preferred_element_type=jnp.float32)
     local_bias = jnp.sum(grad_pre.astype(jnp.float32), axis=0)
     total_msg, total_self, total_bias = lax.psum(
-        (local_msg, local_self, local_bias), ("row", "col")
+        lax.psum((local_msg, local_self, local_bias), "row"), "col"
     )
     factor = 1.0 / math.sqrt(own_rows * row_count * col_count)
     return (

time: 758 us -> 715 us (0.943)
  waiting for transfers between devices: 550 us -> 497 us
  blocking collectives: 78.1 us -> 86.2 us
    psum x1 -> x2, waiting for transfers between devices: 256 us -> 192 us  [the longest x1 130 us: per_device(): lax.psum((local_msg, local_self, local_bias), 'row')]
    reduce_scatter x1, waiting for transfers between devices: 134 us -> 145 us  [per_device(): lax.psum_scatter(back_part.astype(jnp.bfloat16), 'row', scatter_dimension...]
    psum x1 -> x2, blocking collectives: 78.1 us -> 86.2 us  [the longest x1 75.4 us: per_device(): lax.psum((local_msg, local_self, local_bias), 'row')]
  transfers between devices with their start and end apart: 5 -> 6, of which waited for: 5 -> 6; matrix products, arithmetic and copies ran while one was open for 3% -> 3% of each run, Pallas kernels for 0% -> 0%
where the time goes in v1:
time: 715 us; the launch traced here: 712 us
  waiting for transfers between devices  497 us (70%)
  blocking collectives  86.2 us (12%)
  other arithmetic  46.2 us (6%)
  local copies, waits for them, and re-layouts  38.4 us (5%)
  matrix products  29.1 us (4%)
  between operations  14.8 us (2%)
    reduce_scatter x1, waiting for transfers between devices, per_device(): lax.psum_scatter(back_part.astype(jnp.bfloat16), 'row', scatter_dimension...  145 us
    psum x1, waiting for transfers between devices, per_device(): lax.psum((local_msg, local_self, local_bias), 'row')  130 us
    all_gather x1, waiting for transfers between devices, per_device(): column_msgs = lax.all_gather(messages, 'row', axis=0, tiled=True)  101 us
    psum x1, blocking collectives, per_device(): lax.psum((local_msg, local_self, local_bias), 'row')  75.4 us
    psum x1, waiting for transfers between devices, per_device(): lax.psum(lax.psum((local_msg, local_self, local_bias), 'row'), 'col')  62 us
    reduce_scatter x1, waiting for transfers between devices, per_device(): lax.psum_scatter(partial_value.astype(jnp.bfloat16), 'col', scatter_dimen...  30.4 us
    scatter-add x1, other arithmetic, per_device(): jax.ops.segment_sum(backward, slot_cols, num_segments=tile_cols)  29.1 us
    all_gather x1, waiting for transfers between devices, per_device(): grad_rows_all = lax.all_gather(grad_pre, 'col', axis=0, tiled=True)  28.7 us
  transfers between devices with their start and end apart: 6, of which 6 were waited for; matrix products, arithmetic and copies ran while one was open for 3% of the time, Pallas kernels for 0%

profile of v1, /device:TPU:2, one launch (start us, length us, event | category | flops | bytes accessed | tf_op | source)
XLA Modules:
  0.0 712.2 jit_solution(14234278752085636237)
XLA Ops:
  7.2 0.0 copy-start
  7.2 0.0 all-gather.3.cloned.1.call-start
  7.2 0.7 convert_element_type.67
  7.9 0.2 copy-done
  8.1 1.8 fusion.12
  10.0 0.0 all-gather.3.cloned.1.call-update
  10.0 0.0 reduce-scatter.3.cloned.1.call-start
  10.7 0.7 fusion.16
  11.4 100.7 %all-gather.3.cloned.1.call-done = bf16[16384,256]{1,0:T(8,128)(2,1)} async-done(((bf16[512,256]{1,0:T(8,128)(2,1)}), bf16[16384,256]{1,0:T(8,128)(2,1)}) %all-gather.3.cloned.1.call-update) | async-done | bytes 8388624 | tf_op jit(solution)/shard_map/all_gather | solution.py:25
  112.0 9.5 %gather_fusion = bf16[96,128,256]{2,1,0:T(8,128)(2,1)} fusion(bf16[128,128,256]{2,1,0:T(8,128)(2,1)} %bitcast.53, s32[1024]{0:T(1024)S(1)} %pad_clamp_fusion), kind=kCustom, calls=%fused_computation | custom fusion | bytes 12583296 | tf_op jit(solution)/shard_map/gather | solution.py:37
  121.5 0.0 copy-done.2
  121.5 5.5 bitcast_convert_fusion
  127.0 0.0 reduce-scatter.3.cloned.1.call-update
  127.0 0.0 all-gather.5.cloned.1.call-start
  127.1 30.4 %reduce-scatter.3.cloned.1.call-done = bf16[512,256]{1,0:T(8,128)(2,1)} async-done(((bf16[4096,256]{1,0:T(8,128)(2,1)}), bf16[512,256]{1,0:T(8,128)(2,1)}) %reduce-scatter.3.cloned.1.call-update) | async-done | bytes 262160 | tf_op jit(solution)/shard_map/reduce_scatter | solution.py:43
  157.5 0.0 copy-done.6
  157.5 2.3 convert_reduce_fusion
  159.8 0.0 all-gather.5.cloned.1.call-update
  159.8 0.0 reduce-scatter.5.cloned.1.call-start
  159.9 28.7 %all-gather.5.cloned.1.call-done = bf16[4096,256]{1,0:T(8,128)(2,1)} async-done(((bf16[512,256]{1,0:T(8,128)(2,1)}), bf16[4096,256]{1,0:T(8,128)(2,1)}) %all-gather.5.cloned.1.call-update) | async-done | bytes 2097168 | tf_op jit(solution)/shard_map/all_gather | solution.py:48
  188.6 8.0 %convolution_bitcast_fusion = f32[3,32,128,256]{2,3,0,1:T(8,128)} fusion(bf16[32,128,256,1]{2,1,3,0:T(8,128)(2,1)} %bitcast.51, bf16[3,32,128,128]{3,2,1,0:T(8,128)(2,1)S(1)} %bitcast.55, bf16[3,32]{0,1:T(8,128)(2,1)S(1)} %fusion.15), kind=kOutput, calls=%fused_computation.7 | convolution fusion | flops 811597824 | bytes 17825984 | tf_op jit(solution)/shard_map/krij,rif->krjf/dot_general | solution.py:50
  196.6 12.6 %copy.22 = f32[3,32,128,256]{3,2,1,0:T(8,128)} copy(f32[3,32,128,256]{2,3,0,1:T(8,128)} %convolution_bitcast_fusion) | data formatting | bytes 25165824 | tf_op jit(solution)/shard_map/krij,rif->krjf/transpose | solution.py:50
  209.2 7.8 %broadcast_in_dim.2 = f32[128,128,256]{2,1,0:T(8,128)} broadcast(f32[]{:T(128)} %constant.4.clone.1), dimensions={} | broadcast | bytes 16777220 | tf_op jit(solution)/shard_map/broadcast_in_dim | solution.py:53
  217.0 0.0 copy-done.7
  217.0 29.1 %scatter_fusion = f32[128,128,256]{2,1,0:T(8,128)} fusion(f32[128,128,256]{2,1,0:T(8,128)} %broadcast_in_dim.2, s32[96]{0:T(128)S(1)} %bitcast.57, f32[96,128,256]{2,1,0:T(8,128)} %bitcast.46), kind=kCustom, calls=%fused_computation.1 | custom fusion | flops 3145728 | bytes 37749120 | tf_op jit(solution)/shard_map/scatter-add | solution.py:53
  246.1 9.0 %convert_element_type.75 = bf16[128,128,256]{2,1,0:T(8,128)(2,1)} convert(f32[128,128,256]{2,1,0:T(8,128)} %scatter_fusion) | non-fusion elementwise | flops 4194304 | bytes 25165824 | tf_op jit(solution)/shard_map/convert_element_type | solution.py:63
  255.1 0.0 reduce-scatter.5.cloned.1.call-update
  255.2 0.0 all-reduce.5.cloned.1.call-start
  255.2 75.4 %psum.46 = f32[256]{0:T(256)S(1)} all-reduce(f32[256]{0:T(256)S(1)} %get-tuple-element.22), channel_id=1, replica_groups=mesh['row'=32,'col'=8] {'row'}, use_global_device_ids=true, to_apply=%region_8.0 | all-reduce | flops 256 | bytes 2048 | tf_op jit(solution)/shard_map/psum | solution.py:74
  330.7 10.8 %psum.47 = f32[256]{0:T(256)S(1)} all-reduce(f32[256]{0:T(256)S(1)} %psum.46), channel_id=1, replica_groups=mesh['row'=32,'col'=8] {'col'}, use_global_device_ids=true, to_apply=%region_9.0 | all-reduce | flops 256 | bytes 2048 | tf_op jit(solution)/shard_map/psum | solution.py:73
  341.4 0.6 broadcast_multiply_fusion.2
  342.0 0.0 copy-done.3
  342.0 1.0 convolution_bitcast_fusion.1
  343.0 145.1 %reduce-scatter.5.cloned.1.call-done = bf16[512,256]{1,0:T(8,128)(2,1)} async-done(((bf16[16384,256]{1,0:T(8,128)(2,1)}), bf16[512,256]{1,0:T(8,128)(2,1)}) %reduce-scatter.5.cloned.1.call-update) | async-done | bytes 262160 | tf_op jit(solution)/shard_map/reduce_scatter | solution.py:62
  488.1 2.0 convolution_bitcast_fusion.2
  490.1 0.0 all-reduce.5.cloned.1.call-update
  490.1 0.2 all-reduce.7.cloned.1.call-start
  490.4 7.3 %fusion.4 = f32[3,32,128,128]{2,3,0,1:T(8,128)} fusion(bf16[32,128,256,1]{2,1,3,0:T(8,128)(2,1)S(1)} %bitcast.52, bf16[3,32,128,256]{3,2,1,0:T(8,128)(2,1)} %bitcast.49), kind=kOutput, calls=%fused_computation.10 | convolution fusion | flops 805306368 | bytes 14680064 | tf_op jit(solution)/shard_map/rif,krjf->krij/dot_general | solution.py:57
  497.6 6.6 copy.24
  504.2 5.1 multiply_convert_fusion
  509.3 130.0 %all-reduce.5.cloned.1.call-done = (f32[256,256]{0,1:T(8,128)}, f32[256,256]{0,1:T(8,128)}) async-done(((f32[256,256]{0,1:T(8,128)}, f32[256,256]{0,1:T(8,128)}), (f32[256,256]{0,1:T(8,128)}, f32[256,256]{0,1:T(8,128)})) %all-reduce.5.cloned.1.call-update) | async-done | bytes 524304 | tf_op jit(solution)/shard_map/psum | solution.py:74
  639.3 0.0 all-reduce.7.cloned.1.call-update
  639.3 0.3 fusion.14
  639.6 1.0 fusion.13
  640.6 62.0 %all-reduce.7.cloned.1.call-done = (f32[256,256]{0,1:T(8,128)}, f32[256,256]{0,1:T(8,128)}) async-done(((f32[256,256]{0,1:T(8,128)}, f32[256,256]{0,1:T(8,128)}), (f32[256,256]{0,1:T(8,128)}, f32[256,256]{0,1:T(8,128)})) %all-reduce.7.cloned.1.call-update) | async-done | bytes 524304 | tf_op jit(solution)/shard_map/psum | solution.py:73
  702.6 1.1 broadcast_multiply_fusion
  703.7 0.8 copy.26
  704.5 0.8 copy.25
  (13 shorter events, 0.0 us)
Async XLA Ops:
  7.2 1.0 copy-start
  7.2 104.8 %all-gather.3.cloned.1.call-start = ((), (), s32[]{:S(2)}) async-start(), calls=%async_computation.2 | async-start | bytes 8650752 | tf_op jit(solution)/shard_map/all_gather | solution.py:25
  10.0 147.5 %reduce-scatter.3.cloned.1.call-start = ((), (), s32[]{:S(2)}) async-start(), calls=%async_computation.3 | async-start | bytes 2359296 | tf_op jit(solution)/shard_map/reduce_scatter | solution.py:43
  112.0 9.5 %copy-start.2 = (bf16[1,1,96,128,128]{4,3,2,1,0:T(8,128)(2,1)S(1)}, bf16[1,1,96,128,128]{4,3,2,1,0:T(8,128)(2,1)}, u32[]{:S(2)}) copy-start(bf16[1,1,96,128,128]{4,3,2,1,0:T(8,128)(2,1)} %param.16) | copy-start | bytes 9437188
  121.5 36.0 %copy-start.6 = (bf16[256,256]{1,0:T(8,128)(2,1)S(1)}, bf16[256,256]{1,0:T(8,128)(2,1)}, u32[]{:S(2)}) copy-start(bf16[256,256]{1,0:T(8,128)(2,1)} %param.11) | copy-start | bytes 393220
  127.0 61.6 %all-gather.5.cloned.1.call-start = ((), (), s32[]{:S(2)}) async-start(), calls=%async_computation.4 | async-start | bytes 2359296 | tf_op jit(solution)/shard_map/all_gather | solution.py:48
  159.8 328.3 %reduce-scatter.5.cloned.1.call-start = ((), (), s32[]{:S(2)}) async-start(), calls=%async_computation.5 | async-start | bytes 8650752 | tf_op jit(solution)/shard_map/reduce_scatter | solution.py:62
  209.2 7.9 %copy-start.7 = (s32[1,1,96]{2,1,0:T(1,128)S(1)}, s32[1,1,96]{2,1,0:T(1,128)}, u32[]{:S(2)}) copy-start(s32[1,1,96]{2,1,0:T(1,128)} %param.14) | copy-start | bytes 1156
  255.1 86.9 %copy-start.3 = (bf16[512,256]{1,0:T(8,128)(2,1)S(1)}, bf16[512,256]{1,0:T(8,128)(2,1)}, u32[]{:S(2)}) copy-start(bf16[512,256]{1,0:T(8,128)(2,1)} %get-tuple-element.23) | copy-start | bytes 786436
  255.1 235.2 %copy-start.1 = (bf16[4096,256]{1,0:T(8,128)(2,1)S(1)}, bf16[4096,256]{1,0:T(8,128)(2,1)}, u32[]{:S(2)}) copy-start(bf16[4096,256]{1,0:T(8,128)(2,1)} %all-gather.5.cloned.1.call-done) | copy-start | bytes 6291460
  255.2 384.1 %all-reduce.5.cloned.1.call-start = ((), (), s32[]{:S(2)}) async-start(), calls=%async_computation.6 | async-start | bytes 1048576 | tf_op jit(solution)/shard_map/psum | solution.py:74
  490.1 212.5 %all-reduce.7.cloned.1.call-start = ((), (), s32[]{:S(2)}) async-start(), calls=%async_computation.7 | async-start | bytes 1048576 | tf_op jit(solution)/shard_map/psum | solution.py:73
  504.2 135.1 %copy-start.4 = (bf16[512,256]{1,0:T(8,128)(2,1)S(1)}, bf16[512,256]{1,0:T(8,128)(2,1)}, u32[]{:S(2)}) copy-start(bf16[512,256]{1,0:T(8,128)(2,1)} %reduce-scatter.5.cloned.1.call-done) | copy-start | bytes 786436
  504.2 135.1 %copy-start.5 = (bf16[256,256]{1,0:T(8,128)(2,1)S(1)}, bf16[256,256]{1,0:T(8,128)(2,1)}, u32[]{:S(2)}) copy-start(bf16[256,256]{1,0:T(8,128)(2,1)} %param.10) | copy-start | bytes 393220
Sparse Core Ops, SparseCore 0:
  11.1 100.8 all-gather.2
  127.1 30.3 reduce-scatter.2
  159.9 28.6 all-gather.4
  255.3 232.7 reduce-scatter.4
  491.9 147.2 all-reduce.4
  641.5 61.0 all-reduce.6
